TPU v7x, 256 devices: a whole 4x4x8 slice. The times are simulated.
256 devices in a mesh: row: 32 (over z, x_hi, core), col: 8 (over y, x_lo).
Axes of the slice: x: 4 (x_hi: 2, x_lo: 2; x = x_hi * 2 + x_lo), y: 4, z: 8, core: 2. Of those that a mesh axis runs over, the one named last changes fastest.
Arguments:
- object_field: float32 [2, 2, 4096, 1024], P(None, None, 'row', 'col'), may hold values from -1 to 1
- probe: float32 [4, 2, 128, 128], replicated, may hold values from -3 to 3
- kernel_phase: float32 [128, 128], replicated, may hold values from -3.140625 to 3.140625
- amplitudes: float32 [3, 32, 8, 128, 128], P(None, 'row', 'col'), may hold values from 0.05 to 1
- offsets: int32 [3, 32, 8, 2], P(None, 'row', 'col'), may hold values from 0 to 64
Outputs:
- object_out: float32 [2, 2, 4096, 1024], P(None, None, 'row', 'col')
- probe_out: float32 [4, 2, 128, 128], replicated
Inputs may be any that keep to these rules, and one draw needn't show every extreme that they name: offsets[b, r + p, c] place a window of 128 x 128 pixels inside tile (r, c) extended by 32 pixels on each side.
All inputs are finite; a program needn't handle non-finite values.
Results may differ from a plain program's by a relative error of at most 0.0003.
Values sent between devices are 32-bit elements; how exact they have to be, the bound alone decides.
No kernel may reach another device: no remote copies, remote signals or barrier semaphores. Data moves between devices by JAX's collectives and lax.ppermute only.
A program may use at most 128 MiB of HBM per device.

v0:
```python
import math
import jax
import jax.numpy as jnp
from jax import lax
from jax.sharding import PartitionSpec as P

WIN = 128
OVL = 32
SLICES = 2
OBJECT_RATE = 0.5
PROBE_RATE = 0.5
FLOOR = 0.1
HIGHEST = lax.Precision.HIGHEST


def shifted(block, axis, distance):
    devices = range(lax.axis_size(axis))
    route = [(i - distance, i) for i in devices if i - distance in devices]
    return lax.ppermute(block, axis, route)


def filled_up(lines, count):
    spare = -lines.shape[0] % count
    if not spare:
        return lines
    return jnp.concatenate([lines, jnp.zeros((spare, *lines.shape[1:]), lines.dtype)])


def sum_by_parts(x, axis):
    lines = x.reshape(-1, *x.shape[1:][-1:])
    padded = filled_up(lines, lax.axis_size(axis))
    own = lax.psum_scatter(padded, axis, scatter_dimension=0, tiled=True)
    whole = lax.all_gather(own, axis, axis=0, tiled=True)
    return whole[: len(lines)].reshape(x.shape)


def extended_2(cells, sides, width):
    for axis, dim in sides:
        count = lax.axis_size(axis)
        ends = count - 1
        head = lax.slice_in_dim(cells, 0, width, axis=dim)
        tail = lax.slice_in_dim(cells, cells.shape[dim] - width, cells.shape[dim], axis=dim)
        cells = jnp.concatenate(
            [
                lax.ppermute(tail, axis, [(i, (i + 1) % count) for i in range(ends)]),
                cells,
                lax.ppermute(head, axis, [((i + 1) % count, i) for i in range(ends)]),
            ],
            axis=dim,
        )
    return cells


def dft_tables(window):
    counter = jnp.arange(window, dtype=jnp.int32)
    product = counter[:, None] * counter[None, :] % window
    phases = product.astype(jnp.float32) * (-2.0 * math.pi / window)
    scaling = 1.0 / math.sqrt(window)
    return (jnp.cos(phases) * scaling, jnp.sin(phases) * scaling)


def left_apply(matrix, values):
    return jnp.einsum("ij,bjk->bik", matrix, values, precision=HIGHEST)


def right_apply(values, matrix):
    return jnp.einsum("bij,jk->bik", values, matrix, precision=HIGHEST)


def transform(field_pair, tables, inverse):
    cosine, sine = tables
    if inverse:
        sine = -sine
    real_part, imag_part = field_pair
    shape = real_part.shape
    window = shape[-1]
    real_part = real_part.reshape(-1, window, window)
    imag_part = imag_part.reshape(-1, window, window)
    middle_real = left_apply(cosine, real_part) - left_apply(sine, imag_part)
    middle_imag = left_apply(cosine, imag_part) + left_apply(sine, real_part)
    result_real = right_apply(middle_real, cosine) - right_apply(middle_imag, sine)
    result_imag = right_apply(middle_imag, cosine) + right_apply(middle_real, sine)
    return (result_real.reshape(shape), result_imag.reshape(shape))


def complex_product(left_pair, right_pair):
    left_real, left_imag = left_pair
    right_real, right_imag = right_pair
    return (
        left_real * right_real - left_imag * right_imag,
        left_real * right_imag + left_imag * right_real,
    )


def conj_product(left_pair, right_pair):
    left_real, left_imag = left_pair
    right_real, right_imag = right_pair
    return (
        left_real * right_real + left_imag * right_imag,
        left_real * right_imag - left_imag * right_real,
    )


def propagate(field_pair, kernel, tables, adjoint):
    spectrum = transform(field_pair, tables, False)
    phase_pair = (kernel[0], -kernel[1]) if adjoint else kernel
    return transform(complex_product(spectrum, phase_pair), tables, True)


def window_gradients(windows, probe_now, kernel, measured, tables):
    first_slice = (windows[:, 0, 0][:, None], windows[:, 0, 1][:, None])
    second_slice = (windows[:, 1, 0][:, None], windows[:, 1, 1][:, None])
    probe_wave = (probe_now[None, :, 0], probe_now[None, :, 1])
    entrance = complex_product(probe_wave, first_slice)
    spread = propagate(entrance, kernel, tables, False)
    exit_wave = complex_product(spread, second_slice)
    farfield = transform(exit_wave, tables, False)
    intensity = jnp.sum(
        farfield[0] * farfield[0] + farfield[1] * farfield[1], axis=1, keepdims=True
    )
    factor = 1.0 - measured[:, None] / jnp.sqrt(intensity + FLOOR)
    back_second = transform((farfield[0] * factor, farfield[1] * factor), tables, True)
    second_terms = conj_product(spread, back_second)
    grad_second = (jnp.sum(second_terms[0], axis=1), jnp.sum(second_terms[1], axis=1))
    back_first = propagate(conj_product(second_slice, back_second), kernel, tables, True)
    first_terms = conj_product(probe_wave, back_first)
    grad_first = (jnp.sum(first_terms[0], axis=1), jnp.sum(first_terms[1], axis=1))
    probe_terms = conj_product(first_slice, back_first)
    grad_probe = (jnp.sum(probe_terms[0], axis=0), jnp.sum(probe_terms[1], axis=0))
    object_grad = jnp.stack([jnp.stack(grad_first, axis=1), jnp.stack(grad_second, axis=1)], axis=1)
    probe_grad = jnp.stack(grad_probe, axis=1)
    return (object_grad, probe_grad)


def fold_rows(buffer):
    inner = buffer.shape[2] - 2 * OVL
    upper = buffer[:, :, :OVL]
    lower = buffer[:, :, inner + OVL :]
    from_below = shifted(upper, "row", -1)
    from_above = shifted(lower, "row", 1)
    middle = buffer[:, :, OVL : inner + OVL]
    middle = middle.at[:, :, inner - OVL :].add(from_below)
    middle = middle.at[:, :, :OVL].add(from_above)
    return middle


def fold_cols(buffer):
    inner = buffer.shape[3] - 2 * OVL
    leftmost = buffer[:, :, :, :OVL]
    rightmost = buffer[:, :, :, inner + OVL :]
    from_right = shifted(leftmost, "col", -1)
    from_left = shifted(rightmost, "col", 1)
    middle = buffer[:, :, :, OVL : inner + OVL]
    middle = middle.at[:, :, :, inner - OVL :].add(from_right)
    middle = middle.at[:, :, :, :OVL].add(from_left)
    return middle


def probe_total(local_grad):
    partial_sum = sum_by_parts(local_grad, "row")
    return sum_by_parts(partial_sum, "col")


def per_device(object_field, probe, kernel_phase, amplitudes, offsets):
    tables = dft_tables(probe.shape[-1])
    kernel = (jnp.cos(kernel_phase), jnp.sin(kernel_phase))
    devices = lax.axis_size("row") * lax.axis_size("col")
    positions = offsets.shape[1]
    batch_count = offsets.shape[0]
    probe_rate = PROBE_RATE / math.sqrt(devices * positions)
    anchor = jnp.zeros((), jnp.int32)
    window_shape = (SLICES, 2, WIN, WIN)
    current = object_field
    probe_now = probe
    pending = None
    held = None
    for batch_index in range(batch_count):
        extended = extended_2(current, (("row", 2), ("col", 3)), OVL)
        position = 0
        starts = (
            anchor,
            anchor,
            offsets[batch_index, position, 0, 0],
            offsets[batch_index, position, 0, 1],
        )
        start_list = [starts]
        window_list = [lax.dynamic_slice(extended, starts, window_shape)]
        windows = jnp.stack(window_list)
        object_grad, probe_grad = window_gradients(
            windows, probe_now, kernel, amplitudes[batch_index, :, 0], tables
        )
        accumulated = jnp.zeros_like(extended)
        position = 0
        accumulated = lax.dynamic_update_slice(
            accumulated, object_grad[position], start_list[position]
        )
        folded = fold_cols(fold_rows(accumulated))
        current = current - OBJECT_RATE * folded
        if batch_index >= batch_count - 2:
            held = probe_grad if held is None else held + probe_grad
            summed = None
        else:
            summed = probe_total(probe_grad)
        if pending is not None:
            probe_now = probe_now - probe_rate * pending
        pending = summed
    probe_now = probe_now - probe_rate * probe_total(held)
    return (current, probe_now)


def solution(mesh):
    in_specs = (
        P(None, None, "row", "col"),
        P(),
        P(),
        P(None, "row", "col", None, None),
        P(None, "row", "col", None),
    )
    out_specs = (P(None, None, "row", "col"), P())
    return jax.shard_map(
        per_device, mesh=mesh, in_specs=in_specs, out_specs=out_specs, check_vma=False
    )
```

profile of v0, /device:TPU:4, one launch (start us, length us, event | category | flops | bytes accessed | tf_op | source)
XLA Modules:
  0.0 705.8 jit_solution(17390256663919883016)
XLA Ops:
  10.1 5.1 collective-permute-start.1
  27.1 11.6 %collective-permute-done.3 = f32[2,2,192,32]{3,2,1,0:T(8,128)S(1)} collective-permute-done((f32[2,2,192,32]{3,2,1,0:T(8,128)S(1)}, f32[2,2,192,32]{3,2,1,0:T(8,128)S(1)}, u32[]{:S(2)}, u32[]{:S(2)}) %collective-permute-start.3) | collective-permute-done | bytes 98336 | tf_op jit(solution)/shard_map/ppermute | solution.py:47
  86.0 6.1 collective-permute-done.5
  93.7 4.7 collective-permute-start.7
  98.4 5.1 collective-permute-done.6
  107.3 5.1 collective-permute-start.9
  115.3 4.8 collective-permute-start.10
  126.2 12.7 %collective-permute-done.11 = f32[2,2,192,32]{3,2,1,0:T(8,128)S(1)} collective-permute-done((f32[2,2,192,32]{3,2,1,0:T(8,128)S(1)}, f32[2,2,192,32]{3,2,1,0:T(8,128)S(1)}, u32[]{:S(2)}, u32[]{:S(2)}) %collective-permute-start.11) | collective-permute-done | bytes 98336 | tf_op jit(solution)/shard_map/ppermute | solution.py:47
  180.8 3.6 collective-permute-start.12
  187.5 6.1 collective-permute-done.13
  196.9 4.6 collective-permute-start.15
  201.4 3.5 collective-permute-done.14
  207.6 110.5 %reduce-scatter.5.cloned.1.call-done = f32[32,128]{1,0:T(8,128)} async-done(((f32[1024,128]{1,0:T(8,128)}), f32[32,128]{1,0:T(8,128)}) %reduce-scatter.5.cloned.1.call-update) | async-done | bytes 16400 | tf_op jit(solution)/shard_map/reduce_scatter | solution.py:32
  318.1 42.3 %all_gather.12 = f32[1024,128]{1,0:T(8,128)} all-gather(f32[32,128]{1,0:T(8,128)} %reduce-scatter.5.cloned.1.call-done), channel_id=1, replica_groups=mesh['row'=32,'col'=8] {'row'}, dimensions={0}, use_global_device_ids=true | all-gather | bytes 540672 | tf_op jit(solution)/shard_map/all_gather | solution.py:33
  362.7 4.8 collective-permute-start.17
  377.6 6.3 collective-permute-done.18
  383.9 16.4 %collective-permute-done.19 = f32[2,2,192,32]{3,2,1,0:T(8,128)S(1)} collective-permute-done((f32[2,2,192,32]{3,2,1,0:T(8,128)S(1)}, f32[2,2,192,32]{3,2,1,0:T(8,128)S(1)}, u32[]{:S(2)}, u32[]{:S(2)}) %collective-permute-start.19) | collective-permute-done | bytes 98336 | tf_op jit(solution)/shard_map/ppermute | solution.py:47
  403.1 30.0 %all_gather.13 = f32[1024,128]{1,0:T(8,128)S(1)} all-gather(f32[128,128]{1,0:T(8,128)} %reduce-scatter.7.cloned.1.call-done), channel_id=1, replica_groups=mesh['row'=32,'col'=8] {'col'}, dimensions={0}, use_global_device_ids=true | all-gather | bytes 589824 | tf_op jit(solution)/shard_map/all_gather | solution.py:33
  479.8 104.7 %reduce-scatter.9.cloned.1.call-done = f32[32,128]{1,0:T(8,128)} async-done(((f32[1024,128]{1,0:T(8,128)}), f32[32,128]{1,0:T(8,128)}) %reduce-scatter.9.cloned.1.call-update) | async-done | bytes 16400 | tf_op jit(solution)/shard_map/reduce_scatter | solution.py:32
  584.5 42.4 %all_gather.14 = f32[1024,128]{1,0:T(8,128)} all-gather(f32[32,128]{1,0:T(8,128)} %reduce-scatter.9.cloned.1.call-done), channel_id=1, replica_groups=mesh['row'=32,'col'=8] {'row'}, dimensions={0}, use_global_device_ids=true | all-gather | bytes 540672 | tf_op jit(solution)/shard_map/all_gather | solution.py:33
  628.5 4.6 collective-permute-start.23
  633.1 5.1 collective-permute-done.22
  641.5 26.1 %reduce-scatter.11.cloned.1.call-done = f32[128,128]{1,0:T(8,128)} async-done(((f32[1024,128]{1,0:T(8,128)}), f32[128,128]{1,0:T(8,128)}) %reduce-scatter.11.cloned.1.call-update) | async-done | bytes 65552 | tf_op jit(solution)/shard_map/reduce_scatter | solution.py:32
  667.6 30.3 %all_gather.15 = f32[1024,128]{1,0:T(8,128)S(1)} all-gather(f32[128,128]{1,0:T(8,128)} %reduce-scatter.11.cloned.1.call-done), channel_id=1, replica_groups=mesh['row'=32,'col'=8] {'col'}, dimensions={0}, use_global_device_ids=true | all-gather | bytes 589824 | tf_op jit(solution)/shard_map/all_gather | solution.py:33
  (273 shorter events, 182.2 us)
Async XLA Ops:
  7.2 310.9 %reduce-scatter.5.cloned.1.call-start = ((), (), s32[]{:S(2)}) async-start(), calls=%async_computation.4 | async-start | bytes 540672 | tf_op jit(solution)/shard_map/reduce_scatter | solution.py:32
  8.1 8.2 %collective-permute-start = (f32[2,2,32,128]{3,2,1,0:T(8,128)S(1)}, f32[2,2,32,128]{3,2,1,0:T(8,128)S(1)}, u32[]{:S(2)}, u32[]{:S(2)}) collective-permute-start(f32[2,2,32,128]{3,2,1,0:T(8,128)S(1)} %get-tuple-element.209), channel_id=1, source_target_pairs={{0,8},{8,16},{16,24},{24,32},{32,40},{40,48},{48,56},{56,64},{64,7... | collective-permute-start | bytes 196616 | tf_op jit(solution)/shard_map/ppermute | solution.py:45
  10.1 7.0 collective-permute-start.1
  17.3 9.8 %collective-permute-start.2 = (f32[2,2,192,32]{3,2,1,0:T(8,128)S(1)}, f32[2,2,192,32]{3,2,1,0:T(8,128)S(1)}, u32[]{:S(2)}, u32[]{:S(2)}) collective-permute-start(f32[2,2,192,32]{3,2,1,0:T(8,128)S(1)} %get-tuple-element.191), channel_id=1, source_target_pairs={{0,1},{1,2},{2,3},{3,4},{4,5},{5,6},{6,7},{8,9},{9,10},{10,11},{11... | collective-permute-start | bytes 294920 | tf_op jit(solution)/shard_map/ppermute | solution.py:45
  20.4 18.2 %collective-permute-start.3 = (f32[2,2,192,32]{3,2,1,0:T(8,128)S(1)}, f32[2,2,192,32]{3,2,1,0:T(8,128)S(1)}, u32[]{:S(2)}, u32[]{:S(2)}) collective-permute-start(f32[2,2,192,32]{3,2,1,0:T(8,128)S(1)} %get-tuple-element.190), channel_id=1, source_target_pairs={{1,0},{2,1},{3,2},{4,3},{5,4},{6,5},{7,6},{9,8},{10,9},{11,10},{12... | collective-permute-start | bytes 294920 | tf_op jit(solution)/shard_map/ppermute | solution.py:47
  82.9 9.2 %collective-permute-start.5 = (f32[2,2,32,192]{3,2,1,0:T(8,128)S(1)}, f32[2,2,32,192]{3,2,1,0:T(8,128)S(1)}, u32[]{:S(2)}, u32[]{:S(2)}) collective-permute-start(f32[2,2,32,192]{3,2,1,0:T(8,128)S(1)} %get-tuple-element.166), channel_id=1, source_target_pairs={{0,8},{8,16},{16,24},{24,32},{32,40},{40,48},{48,56},{56,64},{64,7... | collective-permute-start | bytes 294920 | tf_op jit(solution)/shard_map/ppermute | solution.py:19
  92.3 11.2 %collective-permute-start.6 = (f32[2,2,128,32]{3,2,1,0:T(8,128)S(1)}, f32[2,2,128,32]{3,2,1,0:T(8,128)S(1)}, u32[]{:S(2)}, u32[]{:S(2)}) collective-permute-start(f32[2,2,128,32]{3,2,1,0:T(8,128)S(1)} %get-tuple-element.185), channel_id=1, source_target_pairs={{1,0},{2,1},{3,2},{4,3},{5,4},{6,5},{7,6},{9,8},{10,9},{11,10},{12... | collective-permute-start | bytes 196616 | tf_op jit(solution)/shard_map/ppermute | solution.py:19
  93.7 11.0 %collective-permute-start.7 = (f32[2,2,128,32]{3,2,1,0:T(8,128)S(1)}, f32[2,2,128,32]{3,2,1,0:T(8,128)S(1)}, u32[]{:S(2)}, u32[]{:S(2)}) collective-permute-start(f32[2,2,128,32]{3,2,1,0:T(8,128)S(1)} %get-tuple-element.184), channel_id=1, source_target_pairs={{0,1},{1,2},{2,3},{3,4},{4,5},{5,6},{6,7},{8,9},{9,10},{10,11},{11... | collective-permute-start | bytes 196616 | tf_op jit(solution)/shard_map/ppermute | solution.py:19
  105.4 7.1 %collective-permute-start.8 = (f32[2,2,32,128]{3,2,1,0:T(8,128)S(1)}, f32[2,2,32,128]{3,2,1,0:T(8,128)S(1)}, u32[]{:S(2)}, u32[]{:S(2)}) collective-permute-start(f32[2,2,32,128]{3,2,1,0:T(8,128)S(1)} %get-tuple-element.202), channel_id=1, source_target_pairs={{0,8},{8,16},{16,24},{24,32},{32,40},{40,48},{48,56},{56,64},{64,7... | collective-permute-start | bytes 196616 | tf_op jit(solution)/shard_map/ppermute | solution.py:45
  107.3 7.0 collective-permute-start.9
  115.3 10.9 %collective-permute-start.10 = (f32[2,2,192,32]{3,2,1,0:T(8,128)}, f32[2,2,192,32]{3,2,1,0:T(8,128)S(1)}, u32[]{:S(2)}, u32[]{:S(2)}) collective-permute-start(f32[2,2,192,32]{3,2,1,0:T(8,128)} %get-tuple-element.189), channel_id=1, source_target_pairs={{0,1},{1,2},{2,3},{3,4},{4,5},{5,6},{6,7},{8,9},{9,10},{10,11},{11... | collective-permute-start | bytes 294920 | tf_op jit(solution)/shard_map/ppermute | solution.py:45
  120.1 18.8 %collective-permute-start.11 = (f32[2,2,192,32]{3,2,1,0:T(8,128)S(1)}, f32[2,2,192,32]{3,2,1,0:T(8,128)S(1)}, u32[]{:S(2)}, u32[]{:S(2)}) collective-permute-start(f32[2,2,192,32]{3,2,1,0:T(8,128)S(1)} %get-tuple-element.188), channel_id=1, source_target_pairs={{1,0},{2,1},{3,2},{4,3},{5,4},{6,5},{7,6},{9,8},{10,9},{11,10},{12... | collective-permute-start | bytes 294920 | tf_op jit(solution)/shard_map/ppermute | solution.py:47
  184.4 9.2 %collective-permute-start.13 = (f32[2,2,32,192]{3,2,1,0:T(8,128)S(1)}, f32[2,2,32,192]{3,2,1,0:T(8,128)S(1)}, u32[]{:S(2)}, u32[]{:S(2)}) collective-permute-start(f32[2,2,32,192]{3,2,1,0:T(8,128)S(1)} %get-tuple-element.164), channel_id=1, source_target_pairs={{0,8},{8,16},{16,24},{24,32},{32,40},{40,48},{48,56},{56,64},{64,7... | collective-permute-start | bytes 294920 | tf_op jit(solution)/shard_map/ppermute | solution.py:19
  194.5 10.5 %collective-permute-start.14 = (f32[2,2,128,32]{3,2,1,0:T(8,128)S(1)}, f32[2,2,128,32]{3,2,1,0:T(8,128)S(1)}, u32[]{:S(2)}, u32[]{:S(2)}) collective-permute-start(f32[2,2,128,32]{3,2,1,0:T(8,128)S(1)} %get-tuple-element.183), channel_id=1, source_target_pairs={{1,0},{2,1},{3,2},{4,3},{5,4},{6,5},{7,6},{9,8},{10,9},{11,10},{12... | collective-permute-start | bytes 196616 | tf_op jit(solution)/shard_map/ppermute | solution.py:19
  196.7 206.4 %reduce-scatter.7.cloned.1.call-start = ((), (), s32[]{:S(2)}) async-start(), calls=%async_computation.5 | async-start | bytes 589824 | tf_op jit(solution)/shard_map/reduce_scatter | solution.py:32
  196.9 10.2 %collective-permute-start.15 = (f32[2,2,128,32]{3,2,1,0:T(8,128)}, f32[2,2,128,32]{3,2,1,0:T(8,128)S(1)}, u32[]{:S(2)}, u32[]{:S(2)}) collective-permute-start(f32[2,2,128,32]{3,2,1,0:T(8,128)} %get-tuple-element.182), channel_id=1, source_target_pairs={{0,1},{1,2},{2,3},{3,4},{4,5},{5,6},{6,7},{8,9},{9,10},{10,11},{11... | collective-permute-start | bytes 196616 | tf_op jit(solution)/shard_map/ppermute | solution.py:19
  360.4 224.1 %reduce-scatter.9.cloned.1.call-start = ((), (), s32[]{:S(2)}) async-start(), calls=%async_computation.6 | async-start | bytes 540672 | tf_op jit(solution)/shard_map/reduce_scatter | solution.py:32
  360.5 7.1 %collective-permute-start.16 = (f32[2,2,32,128]{3,2,1,0:T(8,128)S(1)}, f32[2,2,32,128]{3,2,1,0:T(8,128)S(1)}, u32[]{:S(2)}, u32[]{:S(2)}) collective-permute-start(f32[2,2,32,128]{3,2,1,0:T(8,128)S(1)} %get-tuple-element.196), channel_id=1, source_target_pairs={{0,8},{8,16},{16,24},{24,32},{32,40},{40,48},{48,56},{56,64},{64,7... | collective-permute-start | bytes 196616 | tf_op jit(solution)/shard_map/ppermute | solution.py:45
  369.6 14.2 %collective-permute-start.18 = (f32[2,2,192,32]{3,2,1,0:T(8,128)S(1)}, f32[2,2,192,32]{3,2,1,0:T(8,128)S(1)}, u32[]{:S(2)}, u32[]{:S(2)}) collective-permute-start(f32[2,2,192,32]{3,2,1,0:T(8,128)S(1)} %get-tuple-element.187), channel_id=1, source_target_pairs={{0,1},{1,2},{2,3},{3,4},{4,5},{5,6},{6,7},{8,9},{9,10},{10,11},{11... | collective-permute-start | bytes 294920 | tf_op jit(solution)/shard_map/ppermute | solution.py:45
  372.8 27.5 %collective-permute-start.19 = (f32[2,2,192,32]{3,2,1,0:T(8,128)S(1)}, f32[2,2,192,32]{3,2,1,0:T(8,128)S(1)}, u32[]{:S(2)}, u32[]{:S(2)}) collective-permute-start(f32[2,2,192,32]{3,2,1,0:T(8,128)S(1)} %get-tuple-element.186), channel_id=1, source_target_pairs={{1,0},{2,1},{3,2},{4,3},{5,4},{6,5},{7,6},{9,8},{10,9},{11,10},{12... | collective-permute-start | bytes 294920 | tf_op jit(solution)/shard_map/ppermute | solution.py:47
  471.9 195.7 %reduce-scatter.11.cloned.1.call-start = ((), (), s32[]{:S(2)}) async-start(), calls=%async_computation.7 | async-start | bytes 589824 | tf_op jit(solution)/shard_map/reduce_scatter | solution.py:32
  477.3 149.6 %collective-permute-start.21 = (f32[2,2,32,192]{3,2,1,0:T(8,128)S(1)}, f32[2,2,32,192]{3,2,1,0:T(8,128)S(1)}, u32[]{:S(2)}, u32[]{:S(2)}) collective-permute-start(f32[2,2,32,192]{3,2,1,0:T(8,128)S(1)} %get-tuple-element.162), channel_id=1, source_target_pairs={{0,8},{8,16},{16,24},{24,32},{32,40},{40,48},{48,56},{56,64},{64,7... | collective-permute-start | bytes 294920 | tf_op jit(solution)/shard_map/ppermute | solution.py:19
  627.1 11.1 %collective-permute-start.22 = (f32[2,2,128,32]{3,2,1,0:T(8,128)S(1)}, f32[2,2,128,32]{3,2,1,0:T(8,128)S(1)}, u32[]{:S(2)}, u32[]{:S(2)}) collective-permute-start(f32[2,2,128,32]{3,2,1,0:T(8,128)S(1)} %get-tuple-element.179), channel_id=1, source_target_pairs={{1,0},{2,1},{3,2},{4,3},{5,4},{6,5},{7,6},{9,8},{10,9},{11,10},{12... | collective-permute-start | bytes 196616 | tf_op jit(solution)/shard_map/ppermute | solution.py:19
  628.5 11.8 %collective-permute-start.23 = (f32[2,2,128,32]{3,2,1,0:T(8,128)S(1)}, f32[2,2,128,32]{3,2,1,0:T(8,128)S(1)}, u32[]{:S(2)}, u32[]{:S(2)}) collective-permute-start(f32[2,2,128,32]{3,2,1,0:T(8,128)S(1)} %get-tuple-element.178), channel_id=1, source_target_pairs={{0,1},{1,2},{2,3},{3,4},{4,5},{5,6},{6,7},{8,9},{9,10},{10,11},{11... | collective-permute-start | bytes 196616 | tf_op jit(solution)/shard_map/ppermute | solution.py:19
  (9 other events, 40.0 us)
Sparse Core Ops, SparseCore 0:
  196.8 121.2 reduce-scatter.4
  360.5 42.5 reduce-scatter.6
  472.1 112.3 reduce-scatter.8
  627.0 40.5 reduce-scatter.10
where the time goes:
time: 716 us; the launch traced here: 706 us
  waiting for transfers between devices  325 us (45%)
  blocking collectives  145 us (20%)
  matrix products  111 us (16%)
  starting transfers between devices  70.5 us (10%)
  between operations  27.1 us (4%)
  local copies, waits for them, and re-layouts  24.3 us (3%)
    reduce_scatter x4, waiting for transfers between devices, sum_by_parts(): own = lax.psum_scatter(padded, axis, scatter_dimension=0, tiled=True)  244 us
    all_gather x4, blocking collectives, sum_by_parts(): whole = lax.all_gather(own, axis, axis=0, tiled=True)  145 us
    dot_general x72, matrix products, right_apply(): return jnp.einsum('bij,jk->bik', values, matrix, precision=HIGHEST)  55.8 us
    dot_general x72, matrix products, left_apply(): return jnp.einsum('ij,bjk->bik', matrix, values, precision=HIGHEST)  55.1 us
    ppermute x6, waiting for transfers between devices, extended_2(): lax.ppermute(head, axis, [((i + 1) % count, i) for i in range(ends)])  45.2 us
    ppermute x12, starting transfers between devices, shifted(): return lax.ppermute(block, axis, route)  34.2 us
    ppermute x12, waiting for transfers between devices, shifted(): return lax.ppermute(block, axis, route)  27.6 us
    ppermute x6, starting transfers between devices, extended_2(): lax.ppermute(head, axis, [((i + 1) % count, i) for i in range(ends)])  19 us
  transfers between devices with their start and end apart: 28, of which 20 were waited for; matrix products, arithmetic and copies ran while one was open for 2% of the time, Pallas kernels for 0%

commit v1 on v0

--- a/solution.py
+++ b/solution.py
@@ -30,7 +30,9 @@
     lines = x.reshape(-1, *x.shape[1:][-1:])
     padded = filled_up(lines, lax.axis_size(axis))
     own = lax.psum_scatter(padded, axis, scatter_dimension=0, tiled=True)
-    whole = lax.all_gather(own, axis, axis=0, tiled=True)
+    whole = jnp.concatenate(
+        lax.all_to_all(jnp.stack([own] * lax.axis_size(axis)), axis, 0, 0), axis=0
+    )
     return whole[: len(lines)].reshape(x.shape)
 
 

time: 716 us -> 601 us (0.84)
  blocking collectives: 145 us -> 0 us
  starting transfers between devices: 70.5 us -> 91.6 us
  local copies, waits for them, and re-layouts: 24.3 us -> 32.9 us
    all_gather x4 -> x0, blocking collectives: 145 us -> none  [sum_by_parts(): whole = lax.all_gather(own, axis, axis=0, tiled=True)]
    reduce_scatter x4, waiting for transfers between devices: 244 us -> 221 us  [sum_by_parts(): own = lax.psum_scatter(padded, axis, scatter_dimension=0, tiled=True)]
    all_to_all x0 -> x4, starting transfers between devices: none -> 22 us  [sum_by_parts(): lax.all_to_all(jnp.stack([own] * lax.axis_size(axis)), axis, 0, 0)]
    all_to_all x0 -> x4, waiting for transfers between devices: none -> 19.7 us  [sum_by_parts(): lax.all_to_all(jnp.stack([own] * lax.axis_size(axis)), axis, 0, 0)]
  transfers between devices with their start and end apart: 28 -> 32, of which waited for: 20 -> 22; matrix products, arithmetic and copies ran while one was open for 2% -> 10% of each run, Pallas kernels for 0% -> 0%
where the time goes in v1:
time: 601 us; the launch traced here: 590 us
  waiting for transfers between devices  323 us (54%)
  matrix products  111 us (18%)
  starting transfers between devices  91.6 us (15%)
  local copies, waits for them, and re-layouts  32.9 us (5%)
  between operations  27.1 us (5%)
    reduce_scatter x4, waiting for transfers between devices, sum_by_parts(): own = lax.psum_scatter(padded, axis, scatter_dimension=0, tiled=True)  221 us
    dot_general x72, matrix products, right_apply(): return jnp.einsum('bij,jk->bik', values, matrix, precision=HIGHEST)  55.8 us
    dot_general x72, matrix products, left_apply(): return jnp.einsum('ij,bjk->bik', matrix, values, precision=HIGHEST)  55 us
    ppermute x6, waiting for transfers between devices, extended_2(): lax.ppermute(head, axis, [((i + 1) % count, i) for i in range(ends)])  39.3 us
    ppermute x12, waiting for transfers between devices, shifted(): return lax.ppermute(block, axis, route)  34.1 us
    ppermute x12, starting transfers between devices, shifted(): return lax.ppermute(block, axis, route)  32.6 us
    all_to_all x4, starting transfers between devices, sum_by_parts(): lax.all_to_all(jnp.stack([own] * lax.axis_size(axis)), axis, 0, 0)  22 us
    ppermute x6, starting transfers between devices, extended_2(): lax.ppermute(tail, axis, [(i, (i + 1) % count) for i in range(ends)])  20.5 us
  transfers between devices with their start and end apart: 32, of which 22 were waited for; matrix products, arithmetic and copies ran while one was open for 10% of the time, Pallas kernels for 0%

profile of v1, /device:TPU:4, one launch (start us, length us, event | category | flops | bytes accessed | tf_op | source)
XLA Modules:
  0.0 590.1 jit_solution(2099590124276406625)
XLA Ops:
  10.1 5.1 collective-permute-start.1
  27.1 11.6 %collective-permute-done.3 = f32[2,2,192,32]{3,2,1,0:T(8,128)S(1)} collective-permute-done((f32[2,2,192,32]{3,2,1,0:T(8,128)S(1)}, f32[2,2,192,32]{3,2,1,0:T(8,128)S(1)}, u32[]{:S(2)}, u32[]{:S(2)}) %collective-permute-start.3) | collective-permute-done | bytes 98336 | tf_op jit(solution)/shard_map/ppermute | solution.py:49
  86.8 6.1 %collective-permute-done.5 = f32[2,2,32,192]{3,2,1,0:T(8,128)S(1)} collective-permute-done((f32[2,2,32,192]{3,2,1,0:T(8,128)S(1)}, f32[2,2,32,192]{3,2,1,0:T(8,128)S(1)}, u32[]{:S(2)}, u32[]{:S(2)}) %collective-permute-start.5) | collective-permute-done | bytes 98336 | tf_op jit(solution)/shard_map/ppermute | solution.py:19
  94.5 4.7 collective-permute-start.7
  99.1 5.1 collective-permute-done.6
  108.0 5.1 collective-permute-start.9
  118.0 4.8 collective-permute-start.10
  125.1 5.9 collective-permute-done.10
  131.0 12.7 %collective-permute-done.11 = f32[2,2,192,32]{3,2,1,0:T(8,128)S(1)} collective-permute-done((f32[2,2,192,32]{3,2,1,0:T(8,128)S(1)}, f32[2,2,192,32]{3,2,1,0:T(8,128)S(1)}, u32[]{:S(2)}, u32[]{:S(2)}) %collective-permute-start.11) | collective-permute-done | bytes 98336 | tf_op jit(solution)/shard_map/ppermute | solution.py:49
  186.2 60.4 %reduce-scatter.5.cloned.1.call-done = f32[32,128]{1,0:T(8,128)} async-done(((f32[1024,128]{1,0:T(8,128)}), f32[32,128]{1,0:T(8,128)}) %reduce-scatter.5.cloned.1.call-update) | async-done | bytes 16400 | tf_op jit(solution)/shard_map/reduce_scatter | solution.py:32
  248.2 7.5 %all-to-all-start = ((f32[32,32,128]{2,1,0:T(8,128)}), f32[32,32,128]{2,1,0:T(8,128)S(1)}, u32[]{:S(2)}, u32[]{:S(2)}) async-start(f32[32,32,128]{2,1,0:T(8,128)} %stack.109), calls=%async_computation.1 | async-start | bytes 1048576 | tf_op jit(solution)/shard_map/all_to_all | solution.py:34
  261.9 5.1 collective-permute-done.13
  269.2 4.8 collective-permute-start.15
  278.8 4.9 collective-permute-start.16
  289.9 31.9 %reduce-scatter.7.cloned.1.call-done = f32[128,128]{1,0:T(8,128)} async-done(((f32[1024,128]{1,0:T(8,128)}), f32[128,128]{1,0:T(8,128)}) %reduce-scatter.7.cloned.1.call-update) | async-done | bytes 65552 | tf_op jit(solution)/shard_map/reduce_scatter | solution.py:32
  337.8 10.2 %collective-permute-done.19 = f32[2,2,192,32]{3,2,1,0:T(8,128)S(1)} collective-permute-done((f32[2,2,192,32]{3,2,1,0:T(8,128)S(1)}, f32[2,2,192,32]{3,2,1,0:T(8,128)S(1)}, u32[]{:S(2)}, u32[]{:S(2)}) %collective-permute-start.19) | collective-permute-done | bytes 98336 | tf_op jit(solution)/shard_map/ppermute | solution.py:49
  387.3 114.9 %reduce-scatter.9.cloned.1.call-done = f32[32,128]{1,0:T(8,128)} async-done(((f32[1024,128]{1,0:T(8,128)}), f32[32,128]{1,0:T(8,128)}) %reduce-scatter.9.cloned.1.call-update) | async-done | bytes 16400 | tf_op jit(solution)/shard_map/reduce_scatter | solution.py:32
  503.8 7.5 %all-to-all-start.2 = ((f32[32,32,128]{2,1,0:T(8,128)}), f32[32,32,128]{2,1,0:T(8,128)S(1)}, u32[]{:S(2)}, u32[]{:S(2)}) async-start(f32[32,32,128]{2,1,0:T(8,128)} %stack.250), calls=%async_computation.5 | async-start | bytes 1048576 | tf_op jit(solution)/shard_map/all_to_all | solution.py:34
  516.6 12.4 %all-to-all-done.2 = f32[32,32,128]{2,1,0:T(8,128)S(1)} async-done(((f32[32,32,128]{2,1,0:T(8,128)}), f32[32,32,128]{2,1,0:T(8,128)S(1)}, u32[]{:S(2)}, u32[]{:S(2)}) %all-to-all-start.2) | async-done | bytes 524320 | tf_op jit(solution)/shard_map/all_to_all | solution.py:34
  531.8 5.8 collective-permute-done.21
  539.2 5.5 collective-permute-start.23
  544.7 8.3 %collective-permute-done.22 = f32[2,2,128,32]{3,2,1,0:T(8,128)S(1)} collective-permute-done((f32[2,2,128,32]{3,2,1,0:T(8,128)S(1)}, f32[2,2,128,32]{3,2,1,0:T(8,128)S(1)}, u32[]{:S(2)}, u32[]{:S(2)}) %collective-permute-start.22) | collective-permute-done | bytes 65568 | tf_op jit(solution)/shard_map/ppermute | solution.py:19
  554.4 14.1 %reduce-scatter.11.cloned.1.call-done = f32[128,128]{1,0:T(8,128)} async-done(((f32[1024,128]{1,0:T(8,128)}), f32[128,128]{1,0:T(8,128)}) %reduce-scatter.11.cloned.1.call-update) | async-done | bytes 65552 | tf_op jit(solution)/shard_map/reduce_scatter | solution.py:32
  574.9 7.4 %all-to-all-done.3 = f32[8,128,128]{2,1,0:T(8,128)S(1)} async-done(((f32[8,128,128]{2,1,0:T(8,128)}), f32[8,128,128]{2,1,0:T(8,128)S(1)}, u32[]{:S(2)}, u32[]{:S(2)}) %all-to-all-start.3) | async-done | bytes 524320 | tf_op jit(solution)/shard_map/all_to_all | solution.py:34
  (283 shorter events, 201.2 us)
Async XLA Ops:
  7.2 239.4 %reduce-scatter.5.cloned.1.call-start = ((), (), s32[]{:S(2)}) async-start(), calls=%async_computation.8 | async-start | bytes 540672 | tf_op jit(solution)/shard_map/reduce_scatter | solution.py:32
  17.3 9.8 %collective-permute-start.2 = (f32[2,2,192,32]{3,2,1,0:T(8,128)S(1)}, f32[2,2,192,32]{3,2,1,0:T(8,128)S(1)}, u32[]{:S(2)}, u32[]{:S(2)}) collective-permute-start(f32[2,2,192,32]{3,2,1,0:T(8,128)S(1)} %get-tuple-element.191), channel_id=1, source_target_pairs={{0,1},{1,2},{2,3},{3,4},{4,5},{5,6},{6,7},{8,9},{9,10},{10,11},{11... | collective-permute-start | bytes 294920 | tf_op jit(solution)/shard_map/ppermute | solution.py:47
  20.4 18.2 %collective-permute-start.3 = (f32[2,2,192,32]{3,2,1,0:T(8,128)S(1)}, f32[2,2,192,32]{3,2,1,0:T(8,128)S(1)}, u32[]{:S(2)}, u32[]{:S(2)}) collective-permute-start(f32[2,2,192,32]{3,2,1,0:T(8,128)S(1)} %get-tuple-element.190), channel_id=1, source_target_pairs={{1,0},{2,1},{3,2},{4,3},{5,4},{6,5},{7,6},{9,8},{10,9},{11,10},{12... | collective-permute-start | bytes 294920 | tf_op jit(solution)/shard_map/ppermute | solution.py:49
  83.7 9.2 %collective-permute-start.5 = (f32[2,2,32,192]{3,2,1,0:T(8,128)S(1)}, f32[2,2,32,192]{3,2,1,0:T(8,128)S(1)}, u32[]{:S(2)}, u32[]{:S(2)}) collective-permute-start(f32[2,2,32,192]{3,2,1,0:T(8,128)S(1)} %get-tuple-element.166), channel_id=1, source_target_pairs={{0,8},{8,16},{16,24},{24,32},{32,40},{40,48},{48,56},{56,64},{64,7... | collective-permute-start | bytes 294920 | tf_op jit(solution)/shard_map/ppermute | solution.py:19
  93.0 11.2 %collective-permute-start.6 = (f32[2,2,128,32]{3,2,1,0:T(8,128)S(1)}, f32[2,2,128,32]{3,2,1,0:T(8,128)S(1)}, u32[]{:S(2)}, u32[]{:S(2)}) collective-permute-start(f32[2,2,128,32]{3,2,1,0:T(8,128)S(1)} %get-tuple-element.185), channel_id=1, source_target_pairs={{1,0},{2,1},{3,2},{4,3},{5,4},{6,5},{7,6},{9,8},{10,9},{11,10},{12... | collective-permute-start | bytes 196616 | tf_op jit(solution)/shard_map/ppermute | solution.py:19
  94.5 11.0 %collective-permute-start.7 = (f32[2,2,128,32]{3,2,1,0:T(8,128)S(1)}, f32[2,2,128,32]{3,2,1,0:T(8,128)S(1)}, u32[]{:S(2)}, u32[]{:S(2)}) collective-permute-start(f32[2,2,128,32]{3,2,1,0:T(8,128)S(1)} %get-tuple-element.184), channel_id=1, source_target_pairs={{0,1},{1,2},{2,3},{3,4},{4,5},{5,6},{6,7},{8,9},{9,10},{10,11},{11... | collective-permute-start | bytes 196616 | tf_op jit(solution)/shard_map/ppermute | solution.py:19
  106.1 11.0 %collective-permute-start.8 = (f32[2,2,32,128]{3,2,1,0:T(8,128)S(1)}, f32[2,2,32,128]{3,2,1,0:T(8,128)S(1)}, u32[]{:S(2)}, u32[]{:S(2)}) collective-permute-start(f32[2,2,32,128]{3,2,1,0:T(8,128)S(1)} %get-tuple-element.202), channel_id=1, source_target_pairs={{0,8},{8,16},{16,24},{24,32},{32,40},{40,48},{48,56},{56,64},{64,7... | collective-permute-start | bytes 196616 | tf_op jit(solution)/shard_map/ppermute | solution.py:47
  108.0 9.0 %collective-permute-start.9 = (f32[2,2,32,128]{3,2,1,0:T(8,128)S(1)}, f32[2,2,32,128]{3,2,1,0:T(8,128)S(1)}, u32[]{:S(2)}, u32[]{:S(2)}) collective-permute-start(f32[2,2,32,128]{3,2,1,0:T(8,128)S(1)} %get-tuple-element.203), channel_id=1, source_target_pairs={{8,0},{16,8},{24,16},{32,24},{40,32},{48,40},{56,48},{64,56},{72,6... | collective-permute-start | bytes 196616 | tf_op jit(solution)/shard_map/ppermute | solution.py:49
  118.0 12.9 %collective-permute-start.10 = (f32[2,2,192,32]{3,2,1,0:T(8,128)}, f32[2,2,192,32]{3,2,1,0:T(8,128)S(1)}, u32[]{:S(2)}, u32[]{:S(2)}) collective-permute-start(f32[2,2,192,32]{3,2,1,0:T(8,128)} %get-tuple-element.189), channel_id=1, source_target_pairs={{0,1},{1,2},{2,3},{3,4},{4,5},{5,6},{6,7},{8,9},{9,10},{10,11},{11... | collective-permute-start | bytes 294920 | tf_op jit(solution)/shard_map/ppermute | solution.py:47
  122.9 20.8 %collective-permute-start.11 = (f32[2,2,192,32]{3,2,1,0:T(8,128)S(1)}, f32[2,2,192,32]{3,2,1,0:T(8,128)S(1)}, u32[]{:S(2)}, u32[]{:S(2)}) collective-permute-start(f32[2,2,192,32]{3,2,1,0:T(8,128)S(1)} %get-tuple-element.188), channel_id=1, source_target_pairs={{1,0},{2,1},{3,2},{4,3},{5,4},{6,5},{7,6},{9,8},{10,9},{11,10},{12... | collective-permute-start | bytes 294920 | tf_op jit(solution)/shard_map/ppermute | solution.py:49
  248.2 25.8 %all-to-all-start = ((f32[32,32,128]{2,1,0:T(8,128)}), f32[32,32,128]{2,1,0:T(8,128)S(1)}, u32[]{:S(2)}, u32[]{:S(2)}) async-start(f32[32,32,128]{2,1,0:T(8,128)} %stack.109), calls=%async_computation.1 | async-start | bytes 1048576 | tf_op jit(solution)/shard_map/all_to_all | solution.py:34
  255.7 66.0 %reduce-scatter.7.cloned.1.call-start = ((), (), s32[]{:S(2)}) async-start(), calls=%async_computation.9 | async-start | bytes 589824 | tf_op jit(solution)/shard_map/reduce_scatter | solution.py:32
  257.9 9.0 %collective-permute-start.13 = (f32[2,2,32,192]{3,2,1,0:T(8,128)S(1)}, f32[2,2,32,192]{3,2,1,0:T(8,128)S(1)}, u32[]{:S(2)}, u32[]{:S(2)}) collective-permute-start(f32[2,2,32,192]{3,2,1,0:T(8,128)S(1)} %get-tuple-element.164), channel_id=1, source_target_pairs={{0,8},{8,16},{16,24},{24,32},{32,40},{40,48},{48,56},{56,64},{64,7... | collective-permute-start | bytes 294920 | tf_op jit(solution)/shard_map/ppermute | solution.py:19
  269.2 9.0 %collective-permute-start.15 = (f32[2,2,128,32]{3,2,1,0:T(8,128)}, f32[2,2,128,32]{3,2,1,0:T(8,128)S(1)}, u32[]{:S(2)}, u32[]{:S(2)}) collective-permute-start(f32[2,2,128,32]{3,2,1,0:T(8,128)} %get-tuple-element.182), channel_id=1, source_target_pairs={{0,1},{1,2},{2,3},{3,4},{4,5},{5,6},{6,7},{8,9},{9,10},{10,11},{11... | collective-permute-start | bytes 196616 | tf_op jit(solution)/shard_map/ppermute | solution.py:19
  323.4 25.0 %all-to-all-start.1 = ((f32[8,128,128]{2,1,0:T(8,128)}), f32[8,128,128]{2,1,0:T(8,128)S(1)}, u32[]{:S(2)}, u32[]{:S(2)}) async-start(f32[8,128,128]{2,1,0:T(8,128)} %stack.110), calls=%async_computation.3 | async-start | bytes 1048576 | tf_op jit(solution)/shard_map/all_to_all | solution.py:34
  326.9 175.4 %reduce-scatter.9.cloned.1.call-start = ((), (), s32[]{:S(2)}) async-start(), calls=%async_computation.10 | async-start | bytes 540672 | tf_op jit(solution)/shard_map/reduce_scatter | solution.py:32
  327.9 9.9 %collective-permute-start.18 = (f32[2,2,192,32]{3,2,1,0:T(8,128)}, f32[2,2,192,32]{3,2,1,0:T(8,128)S(1)}, u32[]{:S(2)}, u32[]{:S(2)}) collective-permute-start(f32[2,2,192,32]{3,2,1,0:T(8,128)} %get-tuple-element.187), channel_id=1, source_target_pairs={{0,1},{1,2},{2,3},{3,4},{4,5},{5,6},{6,7},{8,9},{9,10},{10,11},{11... | collective-permute-start | bytes 294920 | tf_op jit(solution)/shard_map/ppermute | solution.py:47
  331.7 16.3 %collective-permute-start.19 = (f32[2,2,192,32]{3,2,1,0:T(8,128)S(1)}, f32[2,2,192,32]{3,2,1,0:T(8,128)S(1)}, u32[]{:S(2)}, u32[]{:S(2)}) collective-permute-start(f32[2,2,192,32]{3,2,1,0:T(8,128)S(1)} %get-tuple-element.186), channel_id=1, source_target_pairs={{1,0},{2,1},{3,2},{4,3},{5,4},{6,5},{7,6},{9,8},{10,9},{11,10},{12... | collective-permute-start | bytes 294920 | tf_op jit(solution)/shard_map/ppermute | solution.py:49
  503.8 25.1 %all-to-all-start.2 = ((f32[32,32,128]{2,1,0:T(8,128)}), f32[32,32,128]{2,1,0:T(8,128)S(1)}, u32[]{:S(2)}, u32[]{:S(2)}) async-start(f32[32,32,128]{2,1,0:T(8,128)} %stack.250), calls=%async_computation.5 | async-start | bytes 1048576 | tf_op jit(solution)/shard_map/all_to_all | solution.py:34
  511.3 57.1 %reduce-scatter.11.cloned.1.call-start = ((), (), s32[]{:S(2)}) async-start(), calls=%async_computation.11 | async-start | bytes 589824 | tf_op jit(solution)/shard_map/reduce_scatter | solution.py:32
  514.7 17.1 %collective-permute-start.20 = (f32[2,2,32,192]{3,2,1,0:T(8,128)S(1)}, f32[2,2,32,192]{3,2,1,0:T(8,128)S(1)}, u32[]{:S(2)}, u32[]{:S(2)}) collective-permute-start(f32[2,2,32,192]{3,2,1,0:T(8,128)S(1)} %get-tuple-element.163), channel_id=1, source_target_pairs={{8,0},{16,8},{24,16},{32,24},{40,32},{48,40},{56,48},{64,56},{72,6... | collective-permute-start | bytes 294920 | tf_op jit(solution)/shard_map/ppermute | solution.py:19
  537.8 15.3 %collective-permute-start.22 = (f32[2,2,128,32]{3,2,1,0:T(8,128)S(1)}, f32[2,2,128,32]{3,2,1,0:T(8,128)S(1)}, u32[]{:S(2)}, u32[]{:S(2)}) collective-permute-start(f32[2,2,128,32]{3,2,1,0:T(8,128)S(1)} %get-tuple-element.179), channel_id=1, source_target_pairs={{1,0},{2,1},{3,2},{4,3},{5,4},{6,5},{7,6},{9,8},{10,9},{11,10},{12... | collective-permute-start | bytes 196616 | tf_op jit(solution)/shard_map/ppermute | solution.py:19
  539.2 34.4 %collective-permute-start.23 = (f32[2,2,128,32]{3,2,1,0:T(8,128)S(1)}, f32[2,2,128,32]{3,2,1,0:T(8,128)S(1)}, u32[]{:S(2)}, u32[]{:S(2)}) collective-permute-start(f32[2,2,128,32]{3,2,1,0:T(8,128)S(1)} %get-tuple-element.178), channel_id=1, source_target_pairs={{0,1},{1,2},{2,3},{3,4},{4,5},{5,6},{6,7},{8,9},{9,10},{10,11},{11... | collective-permute-start | bytes 196616 | tf_op jit(solution)/shard_map/ppermute | solution.py:19
  570.1 12.1 %all-to-all-start.3 = ((f32[8,128,128]{2,1,0:T(8,128)}), f32[8,128,128]{2,1,0:T(8,128)S(1)}, u32[]{:S(2)}, u32[]{:S(2)}) async-start(f32[8,128,128]{2,1,0:T(8,128)} %stack.251), calls=%async_computation.7 | async-start | bytes 1048576 | tf_op jit(solution)/shard_map/all_to_all | solution.py:34
  (14 other events, 73.5 us)
Sparse Core Ops, SparseCore 0:
  125.2 121.3 reduce-scatter.4
  275.0 46.7 reduce-scatter.6
  387.5 114.7 reduce-scatter.8
  529.9 38.4 reduce-scatter.10
